TPU v7x, 32 devices: a whole 2x2x4 slice. The times are simulated.
32 devices in a mesh: parts: 2 (over y), row: 4 (over z), frame: 4 (over x, core).
Axes of the slice: x: 2, y: 2, z: 4, core: 2. Of those that a mesh axis runs over, the one named last changes fastest.
Arguments:
- latent: bfloat16 [8, 8, 16, 512], P(('parts', 'frame'), 'row'), parts along dimension 0, may hold values from -15 to 15
- qkv_weight: bfloat16 [3, 512, 512], P(None, 'frame'), may hold values from -0.125 to 0.125
- out_weight: bfloat16 [512, 512], P('frame'), may hold values from -0.25 to 0.25
- attn_gain: float32 [512], replicated, may hold values from 0.1 to 1.9
- in_weight: bfloat16 [512, 2, 2048], P(None, None, 'frame'), may hold values from -0.25 to 0.25
- depth_weight: float32 [3, 3, 2, 2048], replicated, may hold values from -2 to 2
- down_weight: bfloat16 [2048, 512], P('frame'), may hold values from -0.125 to 0.125
- mlp_gain: float32 [512], replicated, may hold values from 0.1 to 1.9
- conv_first: bfloat16 [3, 3, 3, 512, 512], P(None, None, None, 'frame'), may hold values from -0.0546875 to 0.0546875
- conv_second: bfloat16 [3, 3, 3, 512, 512], P(None, None, None, 'frame'), may hold values from -0.0546875 to 0.0546875
Outputs:
- decoded: bfloat16 [8, 8, 16, 512], P('parts', 'row', 'frame'), parts along dimension 0
There are 2 independent parts, one for each index of `parts`. A program takes and returns all parts, laid end to end along the dimension named above; an argument that names none is the same for every part. Nothing has to cross between parts.
All inputs are finite; a program needn't handle non-finite values.
Results may differ from a plain program's by a relative error of at most 0.015.
Values may be sent and summed in bfloat16 or wider, within the bound.
A program may use at most 128 MiB of HBM per device.

v0:
```python
import jax
import jax.numpy as jnp
from jax import lax
from jax.sharding import PartitionSpec as P

HEAD = 32


def padded_2(cells, sides, width):
    for axis, dim in sides:
        count = lax.axis_size(axis)
        ends = count - 1
        head = lax.slice_in_dim(cells, 0, width, axis=dim)
        tail = lax.slice_in_dim(cells, cells.shape[dim] - width, cells.shape[dim], axis=dim)
        cells = jnp.concatenate(
            [
                lax.ppermute(tail, axis, [(i, (i + 1) % count) for i in range(ends)]),
                cells,
                lax.ppermute(head, axis, [((i + 1) % count, i) for i in range(ends)]),
            ],
            axis=dim,
        )
    return cells


def norm_rows(values, gain):
    return values * lax.rsqrt(jnp.mean(values * values, axis=-1, keepdims=True) + 1e-05) * gain


def attend(packed):
    frames, height, columns = (packed.shape[0], packed.shape[1], packed.shape[2])
    width = packed.shape[4]
    heads = width // HEAD
    flat = packed.reshape(frames, height * columns, 3, heads, HEAD)
    query = jnp.maximum(flat[:, :, 0], 0)
    keys = jnp.maximum(flat[:, :, 1], 0)
    values = flat[:, :, 2]
    state = jnp.einsum("fnhd,fnhe->fhde", keys, values, preferred_element_type=jnp.float32)
    key_total = jnp.sum(keys.astype(jnp.float32), axis=1)
    state, key_total = (
        lax.psum(state.astype(jnp.bfloat16), "row").astype(jnp.float32),
        lax.psum(key_total.astype(jnp.bfloat16), "row").astype(jnp.float32),
    )
    count = height * lax.axis_size("row") * columns
    state = state / count
    key_mean = key_total / count
    query_wide = query.astype(jnp.float32)
    numer = jnp.einsum("fnhd,fhde->fnhe", query_wide, state, precision=lax.Precision.HIGHEST)
    denom = jnp.maximum(
        jnp.einsum("fnhd,fhd->fnh", query_wide, key_mean, precision=lax.Precision.HIGHEST), 1.0
    )
    return (numer / denom[..., None]).astype(jnp.bfloat16).reshape(frames, height, columns, width)


def depth_mix(inner, depth_local):
    height, columns = (inner.shape[1], inner.shape[2])
    extended = padded_2(inner, (("row", 1),), 1)
    padded = jnp.pad(extended, ((0, 0), (0, 0), (1, 1), (0, 0), (0, 0)))
    spread = jnp.zeros(inner.shape, jnp.float32)
    for shift_row in range(3):
        for shift_col in range(3):
            spread = (
                spread
                + padded[:, shift_row : shift_row + height, shift_col : shift_col + columns].astype(
                    jnp.float32
                )
                * depth_local[shift_row, shift_col]
            )
    return (spread[..., 0, :] * jax.nn.silu(spread[..., 1, :])).astype(jnp.bfloat16)


def conv_tile(extended, kernel):
    frames, padded_rows, columns, width = extended.shape
    height = padded_rows - 2
    out_width = kernel.shape[3]
    padded = jnp.pad(extended, ((1, 1), (0, 0), (1, 1), (0, 0)))
    result = jnp.zeros((frames * height * columns, out_width), jnp.float32)
    for shift_time in range(3):
        for shift_row in range(3):
            slab = padded[shift_time : shift_time + frames, shift_row : shift_row + height]
            stacked = jnp.stack(
                [slab[:, :, shift_col : shift_col + columns] for shift_col in range(3)], axis=3
            )
            result = result + jnp.einsum(
                "nci,coi->no",
                stacked.reshape(-1, 3, width),
                kernel[shift_time, shift_row],
                preferred_element_type=jnp.float32,
            )
    return result.reshape(frames, height, columns, out_width)


def local(
    latent,
    qkv_weight,
    out_weight,
    attn_gain,
    in_weight,
    depth_weight,
    down_weight,
    mlp_gain,
    conv_first,
    conv_second,
):
    frames, height, columns, width = latent.shape
    place = lax.axis_index("frame")
    packed = jnp.einsum(
        "frwc,kjc->frwkj",
        latent,
        lax.all_gather(qkv_weight, "frame", axis=1, tiled=True),
        preferred_element_type=jnp.float32,
    ).astype(jnp.bfloat16)
    mixed = attend(packed)
    section = mixed
    attn_out = jnp.einsum(
        "frwj,jc->frwc",
        section,
        lax.all_gather(out_weight, "frame", axis=0, tiled=True),
        preferred_element_type=jnp.float32,
    )
    first = (latent.astype(jnp.float32) + norm_rows(attn_out, attn_gain)).astype(jnp.bfloat16)
    inner = jax.nn.silu(
        jnp.einsum(
            "frwc,ckj->frwkj",
            first,
            lax.all_gather(in_weight, "frame", axis=2, tiled=True),
            preferred_element_type=jnp.float32,
        )
    ).astype(jnp.bfloat16)
    gated = depth_mix(inner, depth_weight)
    section = gated
    mlp_out = jnp.einsum(
        "frwj,jc->frwc",
        section,
        lax.all_gather(down_weight, "frame", axis=0, tiled=True),
        preferred_element_type=jnp.float32,
    )
    second = (first.astype(jnp.float32) + norm_rows(mlp_out, mlp_gain)).astype(jnp.bfloat16)
    gathered = lax.all_gather(second, "frame", axis=0, tiled=True)
    out_share = conv_first.shape[3]
    extended = padded_2(gathered, (("row", 1),), 2)
    activated = jax.nn.silu(conv_tile(extended, conv_first))
    global_row = lax.axis_index("row") * height - 1 + lax.iota(jnp.int32, height + 2)
    inside = ((global_row >= 0) & (global_row < height * lax.axis_size("row"))).astype(jnp.float32)
    hidden_conv = (activated * inside[None, :, None, None]).astype(jnp.bfloat16)
    joined = lax.all_gather(hidden_conv, "frame", axis=3, tiled=True)
    result = conv_tile(joined, conv_second)
    own_part = lax.dynamic_slice_in_dim(gathered, place * out_share, out_share, 3)
    final = (own_part.astype(jnp.float32) + result).astype(jnp.bfloat16)
    return lax.all_to_all(final, "frame", split_axis=2, concat_axis=3, tiled=True)


def solution(mesh):
    in_specs = (
        P(("parts", "frame"), "row", None, None),
        P(None, "frame", None),
        P("frame", None),
        P(),
        P(None, None, "frame"),
        P(),
        P("frame", None),
        P(),
        P(None, None, None, "frame", None),
        P(None, None, None, "frame", None),
    )
    out_specs = P("parts", "row", "frame", None)
    return jax.shard_map(local, mesh=mesh, in_specs=in_specs, out_specs=out_specs, check_vma=False)
```

profile of v0, /device:TPU:0, one launch (start us, length us, event | category | flops | bytes accessed | tf_op | source)
XLA Modules:
  0.0 137.9 jit_solution(649510478248561732)
XLA Ops:
  6.5 0.7 all-gather.4.cloned.1.call-update
  7.3 2.4 %copy.34 = bf16[512,2,512]{2,0,1:T(8,128)(2,1)} copy(bf16[512,2,512]{2,1,0:T(2,128)(2,1)} %param.14) | data formatting | bytes 2097152 | tf_op args[4]
  9.8 0.7 all-gather.8.cloned.1.call-update
  10.5 8.6 %all_gather.19 = bf16[512,512]{1,0:T(8,128)(2,1)S(1)} all-gather(bf16[128,512]{1,0:T(8,128)(2,1)S(1)} %copy-done.1), channel_id=1, replica_groups=mesh['parts'=2,'row'=4,'frame'=4] {'frame'}, dimensions={0}, use_global_device_ids=true | all-gather | bytes 655360 | tf_op jit(solution)/shard_map/all_gather | solution.py:118
  19.1 12.1 %all-gather.4.cloned.1.call-done = bf16[3,512,512]{2,1,0:T(8,128)(2,1)} async-done(((bf16[3,128,512]{2,1,0:T(8,128)(2,1)}), bf16[3,512,512]{2,1,0:T(8,128)(2,1)}) %all-gather.4.cloned.1.call-update) | async-done | bytes 1572880 | tf_op jit(solution)/shard_map/all_gather | solution.py:110
  31.3 2.0 %fusion.7 = bf16[2,16,3,512]{3,1,2,0:T(8,128)(2,1)S(1)} fusion(bf16[3,512,512]{2,1,0:T(8,128)(2,1)} %all-gather.4.cloned.1.call-done, bf16[1,2,16,512]{3,2,1,0:T(8,128)(2,1)S(1)} %copy-done.2), kind=kOutput, calls=%fused_computation.59 | convolution fusion | flops 50380800 | bytes 1703936 | tf_op jit(solution)/shard_map/frwc,kjc->frwkj/dot_general | solution.py:107
  34.0 21.4 %all-reduce.3 = (bf16[1,16,32,32]{3,2,1,0:T(8,128)(2,1)S(1)}, bf16[1,16,32]{2,1,0:T(8,128)(2,1)S(1)}) all-reduce(bf16[1,16,32,32]{3,2,1,0:T(8,128)(2,1)S(1)} %fusion.10, bf16[1,16,32]{2,1,0:T(8,128)(2,1)S(1)} %bitcast.373), channel_id=1, replica_groups=mesh['parts'=2,'row'=4,'frame'=4] {'row'}, use_global_device_ids=true, to_apply=%region_0.0 | all-reduce | flops 16896 | bytes 67584 | tf_op jit(solution)/shard_map/psum | solution.py:41
  55.8 0.4 fusion.28
  56.6 0.3 multiply_reduce_fusion.1
  57.0 10.4 %all-gather.6.cloned.1.call-done = bf16[512,2,2048]{2,0,1:T(8,128)(2,1)} async-done(((bf16[512,2,512]{2,0,1:T(8,128)(2,1)}), bf16[512,2,2048]{2,0,1:T(8,128)(2,1)}) %all-gather.6.cloned.1.call-update) | async-done | bytes 4194320 | tf_op jit(solution)/shard_map/all_gather | solution.py:126
  67.3 3.0 %multiply_convert_fusion = bf16[2,16,2,2048]{3,1,2,0:T(8,128)(2,1)S(1)} fusion(bf16[512,2,2048]{2,0,1:T(8,128)(2,1)} %all-gather.6.cloned.1.call-done, bf16[1,2,16,512]{3,2,1,0:T(8,128)(2,1)S(1)} %fusion.184), kind=kOutput, calls=%fused_computation.154 | convolution fusion | flops 134873088 | bytes 4489216 | tf_op jit(solution)/shard_map/frwc,ckj->frwkj/dot_general | solution.py:123
  70.4 3.4 %collective-permute-start = (bf16[1,1,16,2,2048]{4,2,3,1,0:T(8,128)(2,1)S(1)}, bf16[1,1,16,2,2048]{4,2,3,1,0:T(8,128)(2,1)S(1)}, u32[]{:S(2)}, u32[]{:S(2)}) collective-permute-start(bf16[1,1,16,2,2048]{4,2,3,1,0:T(8,128)(2,1)S(1)} %get-tuple-element.62), channel_id=1, source_target_pairs={{0,4},{4,8},{8,12},{1,5},{5,9},{9,13},{2,6},{6,10},{10,14},{3,7},{... | collective-permute-start | bytes 393224 | tf_op jit(solution)/shard_map/ppermute | solution.py:17
  73.8 1.3 collective-permute-start.1
  75.1 1.8 %collective-permute-done = bf16[1,1,16,2,2048]{4,2,3,1,0:T(8,128)(2,1)S(1)} collective-permute-done((bf16[1,1,16,2,2048]{4,2,3,1,0:T(8,128)(2,1)S(1)}, bf16[1,1,16,2,2048]{4,2,3,1,0:T(8,128)(2,1)S(1)}, u32[]{:S(2)}, u32[]{:S(2)}) %collective-permute-start) | collective-permute-done | bytes 131104 | tf_op jit(solution)/shard_map/ppermute | solution.py:17
  76.9 4.1 %collective-permute-done.1 = bf16[1,1,16,2,2048]{4,2,3,1,0:T(8,128)(2,1)S(1)} collective-permute-done((bf16[1,1,16,2,2048]{4,2,3,1,0:T(8,128)(2,1)S(1)}, bf16[1,1,16,2,2048]{4,2,3,1,0:T(8,128)(2,1)S(1)}, u32[]{:S(2)}, u32[]{:S(2)}) %collective-permute-start.1) | collective-permute-done | bytes 131104 | tf_op jit(solution)/shard_map/ppermute | solution.py:19
  81.1 0.3 fusion.33
  81.3 0.5 fusion.82
  81.8 9.7 %all-gather.8.cloned.1.call-done = bf16[2048,512]{1,0:T(8,128)(2,1)} async-done(((bf16[512,512]{1,0:T(8,128)(2,1)}), bf16[2048,512]{1,0:T(8,128)(2,1)}) %all-gather.8.cloned.1.call-update) | async-done | bytes 2097168 | tf_op jit(solution)/shard_map/all_gather | solution.py:135
  91.5 2.1 %multiply_reduce_fusion = (f32[2,16]{1,0:T(2,128)S(1)}, f32[2,16,512]{2,1,0:T(8,128)S(1)}) fusion(bf16[2048,512]{1,0:T(8,128)(2,1)} %all-gather.8.cloned.1.call-done, f32[1,2,16,2,2048]{4,2,3,1,0:T(8,128)S(1)} %fusion.82), kind=kOutput, calls=%fused_computation.264 | convolution fusion | flops 67534816 | bytes 2687104 | tf_op jit(solution)/shard_map/frwj,jc->frwc/dot_general | solution.py:132
  93.7 5.4 %all_gather.22 = bf16[4,2,16,512]{3,2,1,0:T(8,128)(2,1)S(1)} all-gather(bf16[1,2,16,512]{3,2,1,0:T(8,128)(2,1)S(1)} %fusion.183), channel_id=1, replica_groups=mesh['parts'=2,'row'=4,'frame'=4] {'frame'}, dimensions={0}, use_global_device_ids=true | all-gather | bytes 163840 | tf_op jit(solution)/shard_map/all_gather | solution.py:139
  99.1 3.4 %collective-permute-start.2 = (bf16[4,2,16,512]{3,2,1,0:T(8,128)(2,1)S(1)}, bf16[4,2,16,512]{3,2,1,0:T(8,128)(2,1)S(1)}, u32[]{:S(2)}, u32[]{:S(2)}) collective-permute-start(bf16[4,2,16,512]{3,2,1,0:T(8,128)(2,1)S(1)} %all_gather.22), channel_id=1, source_target_pairs={{0,4},{4,8},{8,12},{1,5},{5,9},{9,13},{2,6},{6,10},{10,14},{3,7},{... | collective-permute-start | bytes 393224 | tf_op jit(solution)/shard_map/ppermute | solution.py:17
  102.5 1.3 collective-permute-start.3
  103.8 1.9 %collective-permute-done.2 = bf16[4,2,16,512]{3,2,1,0:T(8,128)(2,1)S(1)} collective-permute-done((bf16[4,2,16,512]{3,2,1,0:T(8,128)(2,1)S(1)}, bf16[4,2,16,512]{3,2,1,0:T(8,128)(2,1)S(1)}, u32[]{:S(2)}, u32[]{:S(2)}) %collective-permute-start.2) | collective-permute-done | bytes 131104 | tf_op jit(solution)/shard_map/ppermute | solution.py:17
  105.8 4.1 %collective-permute-done.3 = bf16[4,2,16,512]{3,2,1,0:T(8,128)(2,1)S(1)} collective-permute-done((bf16[4,2,16,512]{3,2,1,0:T(8,128)(2,1)S(1)}, bf16[4,2,16,512]{3,2,1,0:T(8,128)(2,1)S(1)}, u32[]{:S(2)}, u32[]{:S(2)}) %collective-permute-start.3) | collective-permute-done | bytes 131104 | tf_op jit(solution)/shard_map/ppermute | solution.py:19
  109.9 0.8 pad_slice_fusion.23
  110.9 1.0 copy-done.5
  111.9 0.4 convolution_bitcast_fusion.8
  112.3 0.4 convolution_bitcast_fusion.7
  112.7 0.4 convolution_bitcast_fusion.6
  113.1 0.4 convolution_bitcast_fusion.5
  113.4 0.4 convolution_bitcast_fusion.4
  113.8 0.4 convolution_bitcast_fusion.3
  114.2 0.4 convolution_bitcast_fusion.2
  114.5 0.4 convolution_bitcast_fusion.1
  114.9 0.4 fusion.18
  115.4 5.9 %all_gather.23 = bf16[4,4,16,512]{3,2,1,0:T(8,128)(2,1)S(1)} all-gather(bf16[4,4,16,128]{3,2,1,0:T(8,128)(2,1)S(1)} %multiply_convert_fusion.1), channel_id=1, replica_groups=mesh['parts'=2,'row'=4,'frame'=4] {'frame'}, dimensions={3}, use_global_device_ids=true | all-gather | bytes 327680 | tf_op jit(solution)/shard_map/all_gather | solution.py:146
  121.3 0.3 pad_slice_fusion.47
  121.8 0.3 convolution_bitcast_fusion.17
  122.1 0.3 convolution_bitcast_fusion.16
  122.4 0.3 convolution_bitcast_fusion.15
  122.6 0.3 convolution_bitcast_fusion.14
  122.9 0.3 convolution_bitcast_fusion.13
  123.2 0.3 convolution_bitcast_fusion.12
  123.5 0.3 convolution_bitcast_fusion.11
  123.7 0.3 convolution_bitcast_fusion.10
  124.0 0.3 fusion.26
  124.4 6.3 %all_to_all.18 = bf16[4,2,16,128]{3,1,0,2:T(2,128)(2,1)S(1)} all-to-all(bf16[4,2,16,128]{3,1,0,2:T(2,128)(2,1)S(1)} %copy.36), channel_id=1, replica_groups=mesh['parts'=2,'row'=4,'frame'=4] {'frame'}, dimensions={2} | all-to-all | bytes 65536 | tf_op jit(solution)/shard_map/all_to_all | solution.py:150
  130.7 0.6 all_to_all.16
  (46 shorter events, 2.3 us)
Async XLA Ops:
  6.5 4.0 %copy-start.1 = (bf16[128,512]{1,0:T(8,128)(2,1)S(1)}, bf16[128,512]{1,0:T(8,128)(2,1)}, u32[]{:S(2)}) copy-start(bf16[128,512]{1,0:T(8,128)(2,1)} %param.12) | copy-start | bytes 393220
  6.5 24.7 %copy-start.2 = (bf16[1,2,16,512]{3,2,1,0:T(8,128)(2,1)S(1)}, bf16[1,2,16,512]{3,2,1,0:T(8,128)(2,1)}, u32[]{:S(2)}) copy-start(bf16[1,2,16,512]{3,2,1,0:T(8,128)(2,1)} %param.10) | copy-start | bytes 98308
  6.5 24.7 %all-gather.4.cloned.1.call-start = ((), (), s32[]{:S(2)}) async-start(), calls=%async_computation.1 | async-start | bytes 1966080 | tf_op jit(solution)/shard_map/all_gather | solution.py:110
  7.3 60.1 %all-gather.6.cloned.1.call-start = ((), (), s32[]{:S(2)}) async-start(), calls=%async_computation.2 | async-start | bytes 5242880 | tf_op jit(solution)/shard_map/all_gather | solution.py:126
  9.7 81.7 %all-gather.8.cloned.1.call-start = ((), (), s32[]{:S(2)}) async-start(), calls=%async_computation.3 | async-start | bytes 2621440 | tf_op jit(solution)/shard_map/all_gather | solution.py:135
  19.1 37.7 %copy-start.3 = (f32[512]{0:T(512)S(1)}, f32[512]{0:T(512)}, u32[]{:S(2)}) copy-start(f32[512]{0:T(512)} %param.13) | copy-start | bytes 6148
  56.9 18.2 %copy-start = (f32[3,3,2,2048]{3,2,1,0:T(2,128)S(1)}, f32[3,3,2,2048]{3,2,1,0:T(2,128)}, u32[]{:S(2)}) copy-start(f32[3,3,2,2048]{3,2,1,0:T(2,128)} %param.15) | copy-start | bytes 442372
  70.4 6.5 %collective-permute-start = (bf16[1,1,16,2,2048]{4,2,3,1,0:T(8,128)(2,1)S(1)}, bf16[1,1,16,2,2048]{4,2,3,1,0:T(8,128)(2,1)S(1)}, u32[]{:S(2)}, u32[]{:S(2)}) collective-permute-start(bf16[1,1,16,2,2048]{4,2,3,1,0:T(8,128)(2,1)S(1)} %get-tuple-element.62), channel_id=1, source_target_pairs={{0,4},{4,8},{8,12},{1,5},{5,9},{9,13},{2,6},{6,10},{10,14},{3,7},{... | collective-permute-start | bytes 393224 | tf_op jit(solution)/shard_map/ppermute | solution.py:17
  73.8 7.3 %collective-permute-start.1 = (bf16[1,1,16,2,2048]{4,2,3,1,0:T(8,128)(2,1)S(1)}, bf16[1,1,16,2,2048]{4,2,3,1,0:T(8,128)(2,1)S(1)}, u32[]{:S(2)}, u32[]{:S(2)}) collective-permute-start(bf16[1,1,16,2,2048]{4,2,3,1,0:T(8,128)(2,1)S(1)} %get-tuple-element.63), channel_id=1, source_target_pairs={{4,0},{8,4},{12,8},{5,1},{9,5},{13,9},{6,2},{10,6},{14,10},{7,3},{... | collective-permute-start | bytes 393224 | tf_op jit(solution)/shard_map/ppermute | solution.py:19
  75.1 18.4 %copy-start.4 = (f32[512]{0:T(512)S(1)}, f32[512]{0:T(512)}, u32[]{:S(2)}) copy-start(f32[512]{0:T(512)} %param.17) | copy-start | bytes 6148
  99.1 6.6 %collective-permute-start.2 = (bf16[4,2,16,512]{3,2,1,0:T(8,128)(2,1)S(1)}, bf16[4,2,16,512]{3,2,1,0:T(8,128)(2,1)S(1)}, u32[]{:S(2)}, u32[]{:S(2)}) collective-permute-start(bf16[4,2,16,512]{3,2,1,0:T(8,128)(2,1)S(1)} %all_gather.22), channel_id=1, source_target_pairs={{0,4},{4,8},{8,12},{1,5},{5,9},{9,13},{2,6},{6,10},{10,14},{3,7},{... | collective-permute-start | bytes 393224 | tf_op jit(solution)/shard_map/ppermute | solution.py:17
  102.5 7.4 %collective-permute-start.3 = (bf16[4,2,16,512]{3,2,1,0:T(8,128)(2,1)S(1)}, bf16[4,2,16,512]{3,2,1,0:T(8,128)(2,1)S(1)}, u32[]{:S(2)}, u32[]{:S(2)}) collective-permute-start(bf16[4,2,16,512]{3,2,1,0:T(8,128)(2,1)S(1)} %all_gather.22), channel_id=1, source_target_pairs={{4,0},{8,4},{12,8},{5,1},{9,5},{13,9},{6,2},{10,6},{14,10},{7,3},{... | collective-permute-start | bytes 393224 | tf_op jit(solution)/shard_map/ppermute | solution.py:19
  109.9 2.0 %copy-start.5 = (bf16[3,3,3,128,512]{4,3,2,1,0:T(8,128)(2,1)S(1)}, bf16[3,3,3,128,512]{4,3,2,1,0:T(8,128)(2,1)}, u32[]{:S(2)}) copy-start(bf16[3,3,3,128,512]{4,3,2,1,0:T(8,128)(2,1)} %param.18) | copy-start | bytes 10616836
  114.9 6.9 %copy-start.6 = (bf16[3,3,3,128,512]{4,3,2,1,0:T(8,128)(2,1)S(1)}, bf16[3,3,3,128,512]{4,3,2,1,0:T(8,128)(2,1)}, u32[]{:S(2)}) copy-start(bf16[3,3,3,128,512]{4,3,2,1,0:T(8,128)(2,1)} %param.19) | copy-start | bytes 10616836
Sparse Core Ops, SparseCore 0:
  8.9 22.3 all-gather.3
  32.8 34.4 all-gather.5
  68.9 22.5 all-gather.7
where the time goes:
time: 138 us
  blocking collectives  47.7 us (35%)
  waiting for transfers between devices  45.5 us (33%)
  matrix products  13.8 us (10%)
  between operations  13.6 us (10%)
  starting transfers between devices  9.45 us (7%)
  local copies, waits for them, and re-layouts  6.56 us (5%)
    psum x1, blocking collectives, attend(): lax.psum(state.astype(jnp.bfloat16), 'row').astype(jnp.float32)  21.4 us
    all_gather x1, waiting for transfers between devices, local(): lax.all_gather(qkv_weight, 'frame', axis=1, tiled=True)  12.1 us
    all_gather x1, waiting for transfers between devices, local(): lax.all_gather(in_weight, 'frame', axis=2, tiled=True)  10.4 us
    all_gather x1, waiting for transfers between devices, local(): lax.all_gather(down_weight, 'frame', axis=0, tiled=True)  9.69 us
    all_gather x1, blocking collectives, local(): lax.all_gather(out_weight, 'frame', axis=0, tiled=True)  8.65 us
    ppermute x2, waiting for transfers between devices, padded_2(): lax.ppermute(head, axis, [((i + 1) % count, i) for i in range(ends)])  8.23 us
    ppermute x2, starting transfers between devices, padded_2(): lax.ppermute(tail, axis, [(i, (i + 1) % count) for i in range(ends)])  6.78 us
    all_to_all x1, blocking collectives, local(): lax.all_to_all(final, 'frame', split_axis=2, concat_axis=3, tiled=True)  6.3 us
  transfers between devices with their start and end apart: 7, of which 7 were waited for; matrix products, arithmetic and copies ran while one was open for 8% of the time, Pallas kernels for 0%

commit v1 on v0

--- a/solution.py
+++ b/solution.py
@@ -4,6 +4,25 @@
 from jax.sharding import PartitionSpec as P
 
 HEAD = 32
+
+
+def in_order(pieces, dim):
+    pieces = jnp.moveaxis(pieces, 0, dim)
+    shape = pieces.shape
+    return pieces.reshape(*shape[:dim], shape[dim] * shape[dim + 1], *shape[dim + 2 :])
+
+
+def work_around(x, axis, dim, work, out_dim):
+    size, position, width = (lax.axis_size(axis), lax.axis_index(axis), x.shape[dim])
+    forward = [(i, (i + 1) % size) for i in range(size)]
+    blocks = []
+    current = x
+    for lap in range(size):
+        coming = current if lap == size - 1 else lax.ppermute(current, axis, forward)
+        blocks.append(work(current, (position - lap) % size * width))
+        current = coming
+    blocks = jnp.stack(blocks)[(position - jnp.arange(size)) % size]
+    return in_order(blocks, out_dim)
 
 
 def padded_2(cells, sides, width):
@@ -104,11 +123,14 @@
 ):
     frames, height, columns, width = latent.shape
     place = lax.axis_index("frame")
-    packed = jnp.einsum(
-        "frwc,kjc->frwkj",
-        latent,
-        lax.all_gather(qkv_weight, "frame", axis=1, tiled=True),
-        preferred_element_type=jnp.float32,
+    packed = work_around(
+        qkv_weight,
+        "frame",
+        1,
+        lambda own_block, offset: jnp.einsum(
+            "frwc,kjc->frwkj", latent, own_block, preferred_element_type=jnp.float32
+        ),
+        4,
     ).astype(jnp.bfloat16)
     mixed = attend(packed)
     section = mixed

time: 138 us -> 139 us (level)
  waiting for transfers between devices: 45.5 us -> 34.2 us
  blocking collectives: 47.7 us -> 58.4 us
    ppermute x0 -> x3, waiting for transfers between devices: none -> 22.5 us  [work_around(): lax.ppermute(current, axis, forward)]
    all_gather x1 -> x0, waiting for transfers between devices: 12.1 us -> none  [local(): lax.all_gather(qkv_weight, 'frame', axis=1, tiled=True)]
    all_gather x1, waiting for transfers between devices: 10.4 us -> 0.02 us  [local(): lax.all_gather(in_weight, 'frame', axis=2, tiled=True)]
    all_gather x1, blocking collectives: 8.65 us -> 18.4 us  [local(): lax.all_gather(out_weight, 'frame', axis=0, tiled=True)]
    all_gather x1, waiting for transfers between devices: 9.69 us -> 0.02 us  [local(): lax.all_gather(down_weight, 'frame', axis=0, tiled=True)]
    ppermute x0 -> x3, starting transfers between devices: none -> 3.02 us  [work_around(): lax.ppermute(current, axis, forward)]
    ppermute x2, starting transfers between devices: 6.78 us -> 5.08 us  [padded_2(): lax.ppermute(tail, axis, [(i, (i + 1) % count) for i in range(ends)])]
    unnamed x19 -> x21, local copies, waits for them, and re-layouts: 3.87 us -> 3.89 us
  transfers between devices with their start and end apart: 7 -> 9, of which waited for: 7 -> 6; matrix products, arithmetic and copies ran while one was open for 8% -> 6% of each run, Pallas kernels for 0% -> 0%
where the time goes in v1:
time: 139 us
  blocking collectives  58.4 us (42%)
  waiting for transfers between devices  34.2 us (25%)
  between operations  13.9 us (10%)
  matrix products  12.9 us (9%)
  starting transfers between devices  10.7 us (8%)
  local copies, waits for them, and re-layouts  7.18 us (5%)
    ppermute x3, waiting for transfers between devices, work_around(): lax.ppermute(current, axis, forward)  22.5 us
    psum x1, blocking collectives, attend(): lax.psum(state.astype(jnp.bfloat16), 'row').astype(jnp.float32)  22.2 us
    all_gather x1, blocking collectives, local(): lax.all_gather(out_weight, 'frame', axis=0, tiled=True)  18.4 us
    ppermute x2, waiting for transfers between devices, padded_2(): lax.ppermute(head, axis, [((i + 1) % count, i) for i in range(ends)])  8.47 us
    all_to_all x1, blocking collectives, local(): lax.all_to_all(final, 'frame', split_axis=2, concat_axis=3, tiled=True)  6.42 us
    all_gather x1, blocking collectives, local(): joined = lax.all_gather(hidden_conv, 'frame', axis=3, tiled=True)  5.94 us
    dot_general x18, matrix products, conv_tile(): jnp.einsum('nci,coi->no', stacked.reshape(-1, 3, width), kernel[shift_tim...  5.74 us
    all_gather x1, blocking collectives, local(): gathered = lax.all_gather(second, 'frame', axis=0, tiled=True)  5.42 us
  transfers between devices with their start and end apart: 9, of which 6 were waited for; matrix products, arithmetic and copies ran while one was open for 6% of the time, Pallas kernels for 0%

profile of v1, /device:TPU:0, one launch (start us, length us, event | category | flops | bytes accessed | tf_op | source)
XLA Modules:
  0.0 138.7 jit_solution(11905137477514892311)
XLA Ops:
  6.5 2.4 %copy.34 = bf16[512,2,512]{2,0,1:T(8,128)(2,1)} copy(bf16[512,2,512]{2,1,0:T(2,128)(2,1)} %param.14) | data formatting | bytes 2097152 | tf_op args[4]
  9.0 0.5 collective-permute-start
  9.8 7.4 %collective-permute-done = bf16[3,128,512]{2,1,0:T(8,128)(2,1)S(1)} collective-permute-done((bf16[3,128,512]{2,1,0:T(8,128)(2,1)}, bf16[3,128,512]{2,1,0:T(8,128)(2,1)S(1)}, u32[]{:S(2)}, u32[]{:S(2)}) %collective-permute-start) | collective-permute-done | bytes 393248 | tf_op jit(solution)/shard_map/ppermute | solution.py:21
  17.3 18.4 %all_gather.15 = bf16[512,512]{1,0:T(8,128)(2,1)S(1)} all-gather(bf16[128,512]{1,0:T(8,128)(2,1)S(1)} %copy-done.3), channel_id=1, replica_groups=mesh['parts'=2,'row'=4,'frame'=4] {'frame'}, dimensions={0}, use_global_device_ids=true | all-gather | bytes 655360 | tf_op jit(solution)/shard_map/all_gather | solution.py:140
  35.6 2.4 %collective-permute-start.2 = (bf16[3,128,512]{2,1,0:T(8,128)(2,1)S(1)}, bf16[3,128,512]{2,1,0:T(8,128)(2,1)S(1)}, u32[]{:S(2)}, u32[]{:S(2)}) collective-permute-start(bf16[3,128,512]{2,1,0:T(8,128)(2,1)S(1)} %collective-permute-done.1), channel_id=1, source_target_pairs={{0,1},{1,2},{2,3},{3,0},{4,5},{5,6},{6,7},{7,4},{8,9},{9,10},{10,1... | collective-permute-start | bytes 1179656 | tf_op jit(solution)/shard_map/ppermute | solution.py:21
  38.6 0.3 convolution_bitcast_fusion.20
  38.8 15.0 %collective-permute-done.2 = bf16[3,128,512]{2,1,0:T(8,128)(2,1)S(1)} collective-permute-done((bf16[3,128,512]{2,1,0:T(8,128)(2,1)S(1)}, bf16[3,128,512]{2,1,0:T(8,128)(2,1)S(1)}, u32[]{:S(2)}, u32[]{:S(2)}) %collective-permute-start.2) | collective-permute-done | bytes 393248 | tf_op jit(solution)/shard_map/ppermute | solution.py:21
  54.2 0.6 gather_fusion
  55.5 22.2 %all-reduce.3 = (bf16[1,16,32,32]{3,2,1,0:T(8,128)(2,1)S(1)}, bf16[1,16,32]{2,1,0:T(8,128)(2,1)S(1)}) all-reduce(bf16[1,16,32,32]{3,2,1,0:T(8,128)(2,1)S(1)} %fusion.5, bf16[1,16,32]{2,1,0:T(8,128)(2,1)S(1)} %bitcast.400), channel_id=1, replica_groups=mesh['parts'=2,'row'=4,'frame'=4] {'row'}, use_global_device_ids=true, to_apply=%region_0.1 | all-reduce | flops 16896 | bytes 67584 | tf_op jit(solution)/shard_map/psum | solution.py:60
  78.2 0.4 fusion.23
  78.9 0.3 multiply_reduce_fusion.1
  79.4 3.1 %multiply_convert_fusion = bf16[2,16,2,2048]{3,1,2,0:T(8,128)(2,1)S(1)} fusion(bf16[512,2,2048]{2,0,1:T(8,128)(2,1)} %all-gather.3.cloned.1.call-done, bf16[1,2,16,512]{3,2,1,0:T(8,128)(2,1)S(1)} %fusion.183), kind=kOutput, calls=%fused_computation.156 | convolution fusion | flops 134873088 | bytes 4489216 | tf_op jit(solution)/shard_map/frwc,ckj->frwkj/dot_general | solution.py:145
  82.5 1.3 collective-permute-start.3
  83.8 1.3 collective-permute-start.4
  85.2 1.2 collective-permute-done.3
  86.3 4.4 %collective-permute-done.4 = bf16[1,1,16,2,2048]{4,2,3,1,0:T(8,128)(2,1)S(1)} collective-permute-done((bf16[1,1,16,2,2048]{4,2,3,1,0:T(8,128)(2,1)S(1)}, bf16[1,1,16,2,2048]{4,2,3,1,0:T(8,128)(2,1)S(1)}, u32[]{:S(2)}, u32[]{:S(2)}) %collective-permute-start.4) | collective-permute-done | bytes 131104 | tf_op jit(solution)/shard_map/ppermute | solution.py:38
  90.7 0.3 fusion.28
  90.9 0.5 fusion.77
  91.5 2.1 %multiply_reduce_fusion = (f32[2,16]{1,0:T(2,128)S(1)}, f32[2,16,512]{2,1,0:T(8,128)S(1)}) fusion(bf16[2048,512]{1,0:T(8,128)(2,1)} %all-gather.5.cloned.1.call-done, f32[1,2,16,2,2048]{4,2,3,1,0:T(8,128)S(1)} %fusion.77), kind=kOutput, calls=%fused_computation.272 | convolution fusion | flops 67534816 | bytes 2687104 | tf_op jit(solution)/shard_map/frwj,jc->frwc/dot_general | solution.py:154
  93.7 5.4 %all_gather.18 = bf16[4,2,16,512]{3,2,1,0:T(8,128)(2,1)S(1)} all-gather(bf16[1,2,16,512]{3,2,1,0:T(8,128)(2,1)S(1)} %fusion.182), channel_id=1, replica_groups=mesh['parts'=2,'row'=4,'frame'=4] {'frame'}, dimensions={0}, use_global_device_ids=true | all-gather | bytes 163840 | tf_op jit(solution)/shard_map/all_gather | solution.py:161
  99.1 3.8 %collective-permute-start.5 = (bf16[4,2,16,512]{3,2,1,0:T(8,128)(2,1)S(1)}, bf16[4,2,16,512]{3,2,1,0:T(8,128)(2,1)S(1)}, u32[]{:S(2)}, u32[]{:S(2)}) collective-permute-start(bf16[4,2,16,512]{3,2,1,0:T(8,128)(2,1)S(1)} %all_gather.18), channel_id=1, source_target_pairs={{0,4},{4,8},{8,12},{1,5},{5,9},{9,13},{2,6},{6,10},{10,14},{3,7},{... | collective-permute-start | bytes 393224 | tf_op jit(solution)/shard_map/ppermute | solution.py:36
  102.9 1.3 collective-permute-start.6
  104.2 1.9 %collective-permute-done.5 = bf16[4,2,16,512]{3,2,1,0:T(8,128)(2,1)S(1)} collective-permute-done((bf16[4,2,16,512]{3,2,1,0:T(8,128)(2,1)S(1)}, bf16[4,2,16,512]{3,2,1,0:T(8,128)(2,1)S(1)}, u32[]{:S(2)}, u32[]{:S(2)}) %collective-permute-start.5) | collective-permute-done | bytes 131104 | tf_op jit(solution)/shard_map/ppermute | solution.py:36
  106.1 4.1 %collective-permute-done.6 = bf16[4,2,16,512]{3,2,1,0:T(8,128)(2,1)S(1)} collective-permute-done((bf16[4,2,16,512]{3,2,1,0:T(8,128)(2,1)S(1)}, bf16[4,2,16,512]{3,2,1,0:T(8,128)(2,1)S(1)}, u32[]{:S(2)}, u32[]{:S(2)}) %collective-permute-start.6) | collective-permute-done | bytes 131104 | tf_op jit(solution)/shard_map/ppermute | solution.py:38
  110.3 0.8 pad_slice_fusion.23
  111.2 1.0 copy-done.6
  112.3 0.4 convolution_bitcast_fusion.8
  112.6 0.4 convolution_bitcast_fusion.7
  113.1 0.4 convolution_bitcast_fusion.6
  113.4 0.4 convolution_bitcast_fusion.5
  113.8 0.4 convolution_bitcast_fusion.4
  114.2 0.4 convolution_bitcast_fusion.3
  114.6 0.4 convolution_bitcast_fusion.2
  114.9 0.4 convolution_bitcast_fusion.1
  115.3 0.4 fusion.13
  115.8 5.9 %all_gather.19 = bf16[4,4,16,512]{3,2,1,0:T(8,128)(2,1)S(1)} all-gather(bf16[4,4,16,128]{3,2,1,0:T(8,128)(2,1)S(1)} %multiply_convert_fusion.1), channel_id=1, replica_groups=mesh['parts'=2,'row'=4,'frame'=4] {'frame'}, dimensions={3}, use_global_device_ids=true | all-gather | bytes 327680 | tf_op jit(solution)/shard_map/all_gather | solution.py:168
  121.7 0.3 pad_slice_fusion.47
  122.2 0.3 convolution_bitcast_fusion.17
  122.5 0.3 convolution_bitcast_fusion.16
  122.8 0.3 convolution_bitcast_fusion.15
  123.0 0.3 convolution_bitcast_fusion.14
  123.3 0.3 convolution_bitcast_fusion.13
  123.6 0.3 convolution_bitcast_fusion.12
  123.9 0.3 convolution_bitcast_fusion.11
  124.1 0.3 convolution_bitcast_fusion.10
  124.4 0.3 fusion.21
  124.8 6.4 %all_to_all.18 = bf16[4,2,16,128]{3,1,0,2:T(2,128)(2,1)S(1)} all-to-all(bf16[4,2,16,128]{3,1,0,2:T(2,128)(2,1)S(1)} %copy.36), channel_id=1, replica_groups=mesh['parts'=2,'row'=4,'frame'=4] {'frame'}, dimensions={2} | all-to-all | bytes 65536 | tf_op jit(solution)/shard_map/all_to_all | solution.py:172
  131.2 0.6 all_to_all.16
  (58 shorter events, 3.3 us)
Async XLA Ops:
  6.5 31.5 %copy-start.1 = (bf16[3,128,512]{2,1,0:T(8,128)(2,1)S(1)}, bf16[3,128,512]{2,1,0:T(8,128)(2,1)}, u32[]{:S(2)}) copy-start(bf16[3,128,512]{2,1,0:T(8,128)(2,1)} %param.11) | copy-start | bytes 1179652
  6.5 10.7 %copy-start.3 = (bf16[128,512]{1,0:T(8,128)(2,1)S(1)}, bf16[128,512]{1,0:T(8,128)(2,1)}, u32[]{:S(2)}) copy-start(bf16[128,512]{1,0:T(8,128)(2,1)} %param.12) | copy-start | bytes 393220
  6.5 31.5 %copy-start = (bf16[1,2,16,512]{3,2,1,0:T(8,128)(2,1)S(1)}, bf16[1,2,16,512]{3,2,1,0:T(8,128)(2,1)}, u32[]{:S(2)}) copy-start(bf16[1,2,16,512]{3,2,1,0:T(8,128)(2,1)} %param.10) | copy-start | bytes 98308
  6.5 72.8 %all-gather.3.cloned.1.call-start = ((), (), s32[]{:S(2)}) async-start(), calls=%async_computation.1 | async-start | bytes 5242880 | tf_op jit(solution)/shard_map/all_gather | solution.py:148
  9.0 82.4 %all-gather.5.cloned.1.call-start = ((), (), s32[]{:S(2)}) async-start(), calls=%async_computation.2 | async-start | bytes 2621440 | tf_op jit(solution)/shard_map/all_gather | solution.py:157
  9.0 8.1 %collective-permute-start = (bf16[3,128,512]{2,1,0:T(8,128)(2,1)}, bf16[3,128,512]{2,1,0:T(8,128)(2,1)S(1)}, u32[]{:S(2)}, u32[]{:S(2)}) collective-permute-start(bf16[3,128,512]{2,1,0:T(8,128)(2,1)} %param.11), channel_id=1, source_target_pairs={{0,1},{1,2},{2,3},{3,0},{4,5},{5,6},{6,7},{7,4},{8,9},{9,10},{10,1... | collective-permute-start | bytes 1179656 | tf_op jit(solution)/shard_map/ppermute | solution.py:21
  17.2 18.5 %collective-permute-start.1 = (bf16[3,128,512]{2,1,0:T(8,128)(2,1)S(1)}, bf16[3,128,512]{2,1,0:T(8,128)(2,1)S(1)}, u32[]{:S(2)}, u32[]{:S(2)}) collective-permute-start(bf16[3,128,512]{2,1,0:T(8,128)(2,1)S(1)} %collective-permute-done), channel_id=1, source_target_pairs={{0,1},{1,2},{2,3},{3,0},{4,5},{5,6},{6,7},{7,4},{8,9},{9,10},{10,1... | collective-permute-start | bytes 1179656 | tf_op jit(solution)/shard_map/ppermute | solution.py:21
  35.6 18.2 %collective-permute-start.2 = (bf16[3,128,512]{2,1,0:T(8,128)(2,1)S(1)}, bf16[3,128,512]{2,1,0:T(8,128)(2,1)S(1)}, u32[]{:S(2)}, u32[]{:S(2)}) collective-permute-start(bf16[3,128,512]{2,1,0:T(8,128)(2,1)S(1)} %collective-permute-done.1), channel_id=1, source_target_pairs={{0,1},{1,2},{2,3},{3,0},{4,5},{5,6},{6,7},{7,4},{8,9},{9,10},{10,1... | collective-permute-start | bytes 1179656 | tf_op jit(solution)/shard_map/ppermute | solution.py:21
  38.3 40.9 %copy-start.4 = (f32[512]{0:T(512)S(1)}, f32[512]{0:T(512)}, u32[]{:S(2)}) copy-start(f32[512]{0:T(512)} %param.13) | copy-start | bytes 6148
  79.3 5.8 %copy-start.2 = (f32[3,3,2,2048]{3,2,1,0:T(2,128)S(1)}, f32[3,3,2,2048]{3,2,1,0:T(2,128)}, u32[]{:S(2)}) copy-start(f32[3,3,2,2048]{3,2,1,0:T(2,128)} %param.15) | copy-start | bytes 442372
  82.5 3.8 %collective-permute-start.3 = (bf16[1,1,16,2,2048]{4,2,3,1,0:T(8,128)(2,1)S(1)}, bf16[1,1,16,2,2048]{4,2,3,1,0:T(8,128)(2,1)S(1)}, u32[]{:S(2)}, u32[]{:S(2)}) collective-permute-start(bf16[1,1,16,2,2048]{4,2,3,1,0:T(8,128)(2,1)S(1)} %get-tuple-element.62), channel_id=1, source_target_pairs={{0,4},{4,8},{8,12},{1,5},{5,9},{9,13},{2,6},{6,10},{10,14},{3,7},{... | collective-permute-start | bytes 393224 | tf_op jit(solution)/shard_map/ppermute | solution.py:36
  83.8 6.9 %collective-permute-start.4 = (bf16[1,1,16,2,2048]{4,2,3,1,0:T(8,128)(2,1)S(1)}, bf16[1,1,16,2,2048]{4,2,3,1,0:T(8,128)(2,1)S(1)}, u32[]{:S(2)}, u32[]{:S(2)}) collective-permute-start(bf16[1,1,16,2,2048]{4,2,3,1,0:T(8,128)(2,1)S(1)} %get-tuple-element.63), channel_id=1, source_target_pairs={{4,0},{8,4},{12,8},{5,1},{9,5},{13,9},{6,2},{10,6},{14,10},{7,3},{... | collective-permute-start | bytes 393224 | tf_op jit(solution)/shard_map/ppermute | solution.py:38
  85.2 8.4 %copy-start.5 = (f32[512]{0:T(512)S(1)}, f32[512]{0:T(512)}, u32[]{:S(2)}) copy-start(f32[512]{0:T(512)} %param.17) | copy-start | bytes 6148
  99.1 7.0 %collective-permute-start.5 = (bf16[4,2,16,512]{3,2,1,0:T(8,128)(2,1)S(1)}, bf16[4,2,16,512]{3,2,1,0:T(8,128)(2,1)S(1)}, u32[]{:S(2)}, u32[]{:S(2)}) collective-permute-start(bf16[4,2,16,512]{3,2,1,0:T(8,128)(2,1)S(1)} %all_gather.18), channel_id=1, source_target_pairs={{0,4},{4,8},{8,12},{1,5},{5,9},{9,13},{2,6},{6,10},{10,14},{3,7},{... | collective-permute-start | bytes 393224 | tf_op jit(solution)/shard_map/ppermute | solution.py:36
  102.9 7.4 %collective-permute-start.6 = (bf16[4,2,16,512]{3,2,1,0:T(8,128)(2,1)S(1)}, bf16[4,2,16,512]{3,2,1,0:T(8,128)(2,1)S(1)}, u32[]{:S(2)}, u32[]{:S(2)}) collective-permute-start(bf16[4,2,16,512]{3,2,1,0:T(8,128)(2,1)S(1)} %all_gather.18), channel_id=1, source_target_pairs={{4,0},{8,4},{12,8},{5,1},{9,5},{13,9},{6,2},{10,6},{14,10},{7,3},{... | collective-permute-start | bytes 393224 | tf_op jit(solution)/shard_map/ppermute | solution.py:38
  110.3 2.0 %copy-start.6 = (bf16[3,3,3,128,512]{4,3,2,1,0:T(8,128)(2,1)S(1)}, bf16[3,3,3,128,512]{4,3,2,1,0:T(8,128)(2,1)}, u32[]{:S(2)}) copy-start(bf16[3,3,3,128,512]{4,3,2,1,0:T(8,128)(2,1)} %param.18) | copy-start | bytes 10616836
  115.3 6.9 %copy-start.7 = (bf16[3,3,3,128,512]{4,3,2,1,0:T(8,128)(2,1)S(1)}, bf16[3,3,3,128,512]{4,3,2,1,0:T(8,128)(2,1)}, u32[]{:S(2)}) copy-start(bf16[3,3,3,128,512]{4,3,2,1,0:T(8,128)(2,1)} %param.19) | copy-start | bytes 10616836
Sparse Core Ops, SparseCore 0:
  9.1 45.7 all-gather.2
  56.4 24.7 all-gather.4
